TPU v7x, 32 devices: a whole 2x2x4 slice. The times are simulated.
32 devices in a mesh: groups: 2 (over y), bx: 4 (over z), by: 2 (over x), bz: 2 (over core).
Axes of the slice: x: 2, y: 2, z: 4, core: 2. Of those that a mesh axis runs over, the one named last changes fastest.
Arguments:
- slab: float32 [4, 512, 1024], P(('groups', 'bz'), 'bx', 'by'), parts along dimension 0, may hold values from -6 to 6
- plane_test: float32 [2, 256], P('bz'), may hold values from -4 to 4
- row_test: float32 [512, 256], P('bx'), may hold values from -0.25 to 0.25
- col_test: float32 [1024, 256], P('by'), may hold values from -0.1875 to 0.1875
- core_planes: float32 [512, 2], P('bz'), may hold values from -4 to 4
- core_rows: float32 [512, 512], P(None, 'bx'), may hold values from -0.25 to 0.25
- core_cols: float32 [512, 1024], P(None, 'by'), may hold values from -0.1875 to 0.1875
Outputs:
- plane_sketch: float32 [4, 256], P(('groups', 'bz')), parts along dimension 0
- row_sketch: float32 [1024, 256], P(('groups', 'bx'), ('by', 'bz')), parts along dimension 0
- col_sketch: float32 [2048, 256], P(('groups', 'by'), ('bx', 'bz')), parts along dimension 0
- core_sketch: float32 [1024, 512, 512], P(('groups', 'bz'), 'bx', 'by'), parts along dimension 0
There are 2 independent parts, one for each index of `groups`. A program takes and returns all parts, laid end to end along the dimension named above; an argument that names none is the same for every part. Nothing has to cross between parts.
All inputs are finite; a program needn't handle non-finite values.
Results may differ from a plain program's by a relative error of at most 0.00011.
Values sent between devices are 32-bit elements; how exact they have to be, the bound alone decides.
A program may use at most 128 MiB of HBM per device.

v0:
```python
import jax
import jax.numpy as jnp
from jax import lax
from jax.sharding import PartitionSpec as P


def on_device(slab, plane_test, row_test, col_test, core_planes, core_rows, core_cols):
    highest = lax.Precision.HIGHEST
    by_col = jnp.einsum("pij,jr->pir", slab, col_test, precision=highest)
    plane_part = jnp.einsum("pir,ir->pr", by_col, row_test, precision=highest)
    row_part = jnp.einsum("pir,pr->ir", by_col, plane_test, precision=highest)
    by_row = jnp.einsum("pij,ir->pjr", slab, row_test, precision=highest)
    col_part = jnp.einsum("pjr,pr->jr", by_row, plane_test, precision=highest)
    plane_sketch = lax.psum(plane_part, ("bx", "by"))
    row_sketch = lax.psum_scatter(row_part, ("by", "bz"), scatter_dimension=1, tiled=True)
    col_sketch = lax.psum_scatter(col_part, ("bx", "bz"), scatter_dimension=1, tiled=True)
    shrunk = jnp.einsum("pij,bj->pib", slab, core_cols, precision=highest)
    reduced = lax.psum_scatter(shrunk, "by", scatter_dimension=2, tiled=True)
    partial_value = jnp.einsum("pib,ai->pab", reduced, core_rows, precision=highest)
    partial_value = lax.psum_scatter(partial_value, "bx", scatter_dimension=1, tiled=True)
    core_sketch = jnp.einsum(
        "cp,pab->cab",
        core_planes,
        lax.all_gather(partial_value, "bz", axis=0, tiled=True),
        precision=highest,
    )
    return (plane_sketch, row_sketch, col_sketch, core_sketch)


def solution(mesh):
    in_specs = (
        P(("groups", "bz"), "bx", "by"),
        P("bz", None),
        P("bx", None),
        P("by", None),
        P("bz", None),
        P(None, "bx"),
        P(None, "by"),
    )
    out_specs = (
        P(("groups", "bz"), None),
        P(("groups", "bx"), ("by", "bz")),
        P(("groups", "by"), ("bx", "bz")),
        P(("groups", "bz"), "bx", "by"),
    )
    return jax.shard_map(
        on_device, mesh=mesh, in_specs=in_specs, out_specs=out_specs, check_vma=False
    )
```

profile of v0, /device:TPU:0, one launch (start us, length us, event | category | flops | bytes accessed | tf_op | source)
XLA Modules:
  0.0 129.5 jit_solution(7191022147818254434)
XLA Ops:
  7.2 0.0 copy-start
  7.2 0.0 reduce-scatter.9.cloned.1.call-start
  7.2 1.2 copy-done
  8.4 2.8 %convolution_bitcast_fusion.2 = f32[1,128,512]{2,1,0:T(8,128)} fusion(f32[512,512]{1,0:T(8,128)S(1)} %copy-done, f32[1,128,512]{2,1,0:T(8,128)} %param.7), kind=kOutput, calls=%fused_computation.4 | convolution fusion | flops 402653184 | bytes 1572864 | tf_op jit(solution)/shard_map/pij,bj->pib/dot_general | solution.py:17
  11.2 0.0 reduce-scatter.9.cloned.1.call-update
  11.2 0.0 reduce-scatter.11.cloned.1.call-start
  11.3 14.5 %reduce-scatter.9.cloned.1.call-done = f32[1,128,256]{2,1,0:T(8,128)} async-done(((f32[1,128,512]{2,1,0:T(8,128)}), f32[1,128,256]{2,1,0:T(8,128)}) %reduce-scatter.9.cloned.1.call-update) | async-done | bytes 131088 | tf_op jit(solution)/shard_map/reduce_scatter | solution.py:18
  25.8 2.4 %convolution_bitcast_fusion.1 = f32[1,512,256]{1,2,0:T(8,128)} fusion(f32[512,128]{1,0:T(8,128)} %param.12, f32[1,128,256]{2,1,0:T(8,128)} %reduce-scatter.9.cloned.1.call-done), kind=kOutput, calls=%fused_computation.1 | convolution fusion | flops 201326592 | bytes 917504 | tf_op jit(solution)/shard_map/pib,ai->pab/dot_general | solution.py:19
  28.2 0.0 reduce-scatter.11.cloned.1.call-update
  28.2 0.0 reduce-scatter.13.cloned.1.call-start
  28.3 1.6 %multiply_reduce_fusion = (f32[256]{0:T(256)S(1)}, f32[128,256]{1,0:T(8,128)S(1)}) fusion(f32[128,256]{1,0:T(8,128)} %param.9, f32[512,256]{1,0:T(8,128)} %param.10, f32[1,128,512]{2,1,0:T(8,128)} %param.7), kind=kOutput, calls=%fused_computation.11 | convolution fusion | flops 201391872 | bytes 1049600 | tf_op jit(solution)/shard_map/pij,jr->pir/dot_general | solution.py:9
  29.9 0.7 broadcast_multiply_fusion
  30.5 0.7 copy.24
  31.3 0.0 reduce-scatter.13.cloned.1.call-update
  31.3 0.0 reduce-scatter.7.cloned.1.call-start
  31.4 2.4 %fusion = f32[512,256]{0,1:T(8,128)} fusion(f32[128,256]{1,0:T(8,128)} %param.9, f32[1,128,512]{2,1,0:T(8,128)} %param.7, f32[256]{0:T(256)} %bitcast.40), kind=kOutput, calls=%fused_computation.3 | convolution fusion | flops 201457664 | bytes 918528 | tf_op jit(solution)/shard_map/pij,ir->pjr/dot_general | solution.py:12
  33.8 0.0 reduce-scatter.7.cloned.1.call-update
  33.8 21.1 %psum.7 = f32[1,256]{1,0:T(1,128)} all-reduce(f32[1,256]{1,0:T(1,128)S(1)} %bitcast.38), channel_id=1, replica_groups=mesh['groups'=2,'bx'=4,'by'=2,'bz'=2] {'bx','by'}, use_global_device_ids=true, to_apply=%region_0.0 | all-reduce | flops 256 | bytes 2048 | tf_op jit(solution)/shard_map/psum | solution.py:14
  54.9 0.0 reduce-scatter.11.cloned.1.call-done
  54.9 1.0 copy.14
  55.9 2.0 %all_gather.3 = f32[2,128,256]{2,1,0:T(8,128)S(1)} all-gather(f32[1,128,256]{2,1,0:T(8,128)S(1)} %copy.14), channel_id=1, replica_groups=mesh['groups'=2,'bx'=4,'by'=2,'bz'=2] {'bz'}, dimensions={0}, use_global_device_ids=true | all-gather | bytes 393216 | tf_op jit(solution)/shard_map/all_gather | solution.py:24
  57.9 0.0 copy-start.1
  57.9 30.9 %convolution_bitcast_fusion = f32[256,128,256]{0,2,1:T(8,128)} fusion(f32[2,128,256]{2,1,0:T(8,128)S(1)} %all_gather.3, f32[256,2]{0,1:T(2,128)} %param.11), kind=kOutput, calls=%fused_computation | convolution fusion | flops 201326592 | bytes 33818624 | tf_op jit(solution)/shard_map/cp,pab->cab/dot_general | solution.py:21
  88.8 34.1 %copy.17 = f32[256,128,256]{2,1,0:T(8,128)} copy(f32[256,128,256]{0,2,1:T(8,128)} %convolution_bitcast_fusion) | data formatting | bytes 67108864
  122.9 0.0 reduce-scatter.13.cloned.1.call-done
  122.9 0.0 reduce-scatter.7.cloned.1.call-done
  122.9 0.0 copy-done.1
Async XLA Ops:
  7.2 1.2 copy-start
  7.2 18.6 %reduce-scatter.9.cloned.1.call-start = ((), (), s32[]{:S(2)}) async-start(), calls=%async_computation.5 | async-start | bytes 393216 | tf_op jit(solution)/shard_map/reduce_scatter | solution.py:18
  11.2 43.6 %reduce-scatter.11.cloned.1.call-start = ((), (), s32[]{:S(2)}) async-start(), calls=%async_computation.6 | async-start | bytes 655360 | tf_op jit(solution)/shard_map/reduce_scatter | solution.py:20
  28.2 94.7 %reduce-scatter.13.cloned.1.call-start = ((), (), s32[]{:S(2)}) async-start(), calls=%async_computation.7 | async-start | bytes 163840
  31.3 91.6 %reduce-scatter.7.cloned.1.call-start = ((), (), s32[]{:S(2)}) async-start(), calls=%async_computation.4 | async-start | bytes 589824 | tf_op jit(solution)/shard_map/reduce_scatter | solution.py:16
  57.9 65.0 %copy-start.1 = (f32[512,512]{1,0:T(8,128)S(1)}, f32[512,512]{1,0:T(8,128)}, u32[]{:S(2)}) copy-start(f32[512,512]{1,0:T(8,128)} %param.13) | copy-start | bytes 3145732
Sparse Core Ops, SparseCore 0:
  11.4 14.3 reduce-scatter.8
  28.7 21.6 reduce-scatter.10
  53.5 17.8 reduce-scatter.12
  74.2 30.9 reduce-scatter.6
where the time goes:
time: 130 us; the launch traced here: 129 us
  matrix products  40.2 us (31%)
  local copies, waits for them, and re-layouts  37 us (28%)
  blocking collectives  23.1 us (18%)
  waiting for transfers between devices  14.5 us (11%)
  between operations  13.8 us (11%)
    unnamed x6, local copies, waits for them, and re-layouts  36 us
    dot_general x1, matrix products, on_device(): jnp.einsum('cp,pab->cab', core_planes, lax.all_gather(partial_value, 'bz'...  30.9 us
    psum x1, blocking collectives, on_device(): plane_sketch = lax.psum(plane_part, ('bx', 'by'))  21.1 us
    reduce_scatter x1, waiting for transfers between devices, on_device(): reduced = lax.psum_scatter(shrunk, 'by', scatter_dimension=2, tiled=True)  14.5 us
    dot_general x1, matrix products, on_device(): shrunk = jnp.einsum('pij,bj->pib', slab, core_cols, precision=highest)  2.83 us
  transfers between devices with their start and end apart: 4, of which 1 were waited for; matrix products, arithmetic and copies ran while one was open for 55% of the time, Pallas kernels for 0%

commit v1 on v0

--- a/solution.py
+++ b/solution.py
@@ -11,7 +11,8 @@
     row_part = jnp.einsum("pir,pr->ir", by_col, plane_test, precision=highest)
     by_row = jnp.einsum("pij,ir->pjr", slab, row_test, precision=highest)
     col_part = jnp.einsum("pjr,pr->jr", by_row, plane_test, precision=highest)
-    plane_sketch = lax.psum(plane_part, ("bx", "by"))
+    partial = lax.psum(plane_part, "by")
+    plane_sketch = lax.psum(partial, "bx")
     row_sketch = lax.psum_scatter(row_part, ("by", "bz"), scatter_dimension=1, tiled=True)
     col_sketch = lax.psum_scatter(col_part, ("bx", "bz"), scatter_dimension=1, tiled=True)
     shrunk = jnp.einsum("pij,bj->pib", slab, core_cols, precision=highest)

time: 130 us -> 127 us (0.977)
  blocking collectives: 23.1 us -> 19.5 us
    psum x1 -> x2, blocking collectives: 21.1 us -> 17.5 us  [the longest x1 12.6 us: on_device(): plane_sketch = lax.psum(partial, 'bx')]
  transfers between devices with their start and end apart: 4 -> 4, of which waited for: 1 -> 1; matrix products, arithmetic and copies ran while one was open for 55% -> 57% of each run, Pallas kernels for 0% -> 0%
where the time goes in v1:
time: 127 us; the launch traced here: 126 us
  matrix products  40.2 us (32%)
  local copies, waits for them, and re-layouts  37.1 us (29%)
  blocking collectives  19.5 us (15%)
  waiting for transfers between devices  14.5 us (11%)
  between operations  13.8 us (11%)
    unnamed x6, local copies, waits for them, and re-layouts  36.1 us
    dot_general x1, matrix products, on_device(): jnp.einsum('cp,pab->cab', core_planes, lax.all_gather(partial_value, 'bz'...  30.9 us
    reduce_scatter x1, waiting for transfers between devices, on_device(): reduced = lax.psum_scatter(shrunk, 'by', scatter_dimension=2, tiled=True)  14.5 us
    psum x1, blocking collectives, on_device(): plane_sketch = lax.psum(partial, 'bx')  12.6 us
    psum x1, blocking collectives, on_device(): partial = lax.psum(plane_part, 'by')  4.94 us
    dot_general x1, matrix products, on_device(): shrunk = jnp.einsum('pij,bj->pib', slab, core_cols, precision=highest)  2.83 us
  transfers between devices with their start and end apart: 4, of which 1 were waited for; matrix products, arithmetic and copies ran while one was open for 57% of the time, Pallas kernels for 0%

profile of v1, /device:TPU:0, one launch (start us, length us, event | category | flops | bytes accessed | tf_op | source)
XLA Modules:
  0.0 126.0 jit_solution(11391477965267706261)
XLA Ops:
  7.2 0.0 copy-start
  7.2 0.0 reduce-scatter.9.cloned.1.call-start
  7.2 1.2 copy-done
  8.4 2.8 %convolution_bitcast_fusion.2 = f32[1,128,512]{2,1,0:T(8,128)} fusion(f32[512,512]{1,0:T(8,128)S(1)} %copy-done, f32[1,128,512]{2,1,0:T(8,128)} %param.7), kind=kOutput, calls=%fused_computation.4 | convolution fusion | flops 402653184 | bytes 1572864 | tf_op jit(solution)/shard_map/pij,bj->pib/dot_general | solution.py:18
  11.2 0.0 reduce-scatter.9.cloned.1.call-update
  11.2 0.0 reduce-scatter.11.cloned.1.call-start
  11.3 14.5 %reduce-scatter.9.cloned.1.call-done = f32[1,128,256]{2,1,0:T(8,128)} async-done(((f32[1,128,512]{2,1,0:T(8,128)}), f32[1,128,256]{2,1,0:T(8,128)}) %reduce-scatter.9.cloned.1.call-update) | async-done | bytes 131088 | tf_op jit(solution)/shard_map/reduce_scatter | solution.py:19
  25.8 2.4 %convolution_bitcast_fusion.1 = f32[1,512,256]{1,2,0:T(8,128)} fusion(f32[512,128]{1,0:T(8,128)} %param.12, f32[1,128,256]{2,1,0:T(8,128)} %reduce-scatter.9.cloned.1.call-done), kind=kOutput, calls=%fused_computation.1 | convolution fusion | flops 201326592 | bytes 917504 | tf_op jit(solution)/shard_map/pib,ai->pab/dot_general | solution.py:20
  28.2 0.0 reduce-scatter.11.cloned.1.call-update
  28.2 0.0 reduce-scatter.13.cloned.1.call-start
  28.3 1.6 %multiply_reduce_fusion = (f32[256]{0:T(256)S(1)}, f32[128,256]{1,0:T(8,128)S(1)}) fusion(f32[128,256]{1,0:T(8,128)} %param.9, f32[512,256]{1,0:T(8,128)} %param.10, f32[1,128,512]{2,1,0:T(8,128)} %param.7), kind=kOutput, calls=%fused_computation.11 | convolution fusion | flops 201391872 | bytes 1049600 | tf_op jit(solution)/shard_map/pij,jr->pir/dot_general | solution.py:9
  29.9 0.7 broadcast_multiply_fusion
  30.5 0.7 copy.24
  31.3 0.0 reduce-scatter.13.cloned.1.call-update
  31.3 0.0 reduce-scatter.7.cloned.1.call-start
  31.4 2.4 %fusion = f32[512,256]{0,1:T(8,128)} fusion(f32[128,256]{1,0:T(8,128)} %param.9, f32[1,128,512]{2,1,0:T(8,128)} %param.7, f32[256]{0:T(256)} %bitcast.40), kind=kOutput, calls=%fused_computation.3 | convolution fusion | flops 201457664 | bytes 918528 | tf_op jit(solution)/shard_map/pij,ir->pjr/dot_general | solution.py:12
  33.8 0.0 reduce-scatter.7.cloned.1.call-update
  33.8 4.9 %psum.14 = f32[1,256]{1,0:T(1,128)S(1)} all-reduce(f32[1,256]{1,0:T(1,128)S(1)} %bitcast.38), channel_id=1, replica_groups=mesh['groups'=2,'bx'=4,'by'=2,'bz'=2] {'by'}, use_global_device_ids=true, to_apply=%region_0.0 | all-reduce | flops 256 | bytes 2048 | tf_op jit(solution)/shard_map/psum | solution.py:14
  38.7 12.6 %psum.15 = f32[1,256]{1,0:T(1,128)} all-reduce(f32[1,256]{1,0:T(1,128)S(1)} %psum.14), channel_id=1, replica_groups=mesh['groups'=2,'bx'=4,'by'=2,'bz'=2] {'bx'}, use_global_device_ids=true, to_apply=%region_1.0 | all-reduce | flops 256 | bytes 2048 | tf_op jit(solution)/shard_map/psum | solution.py:15
  51.3 0.0 reduce-scatter.11.cloned.1.call-done
  51.3 1.0 copy.14
  52.3 2.0 %all_gather.3 = f32[2,128,256]{2,1,0:T(8,128)S(1)} all-gather(f32[1,128,256]{2,1,0:T(8,128)S(1)} %copy.14), channel_id=1, replica_groups=mesh['groups'=2,'bx'=4,'by'=2,'bz'=2] {'bz'}, dimensions={0}, use_global_device_ids=true | all-gather | bytes 393216 | tf_op jit(solution)/shard_map/all_gather | solution.py:25
  54.3 0.0 copy-start.1
  54.3 30.9 %convolution_bitcast_fusion = f32[256,128,256]{0,2,1:T(8,128)} fusion(f32[2,128,256]{2,1,0:T(8,128)S(1)} %all_gather.3, f32[256,2]{0,1:T(2,128)} %param.11), kind=kOutput, calls=%fused_computation | convolution fusion | flops 201326592 | bytes 33818624 | tf_op jit(solution)/shard_map/cp,pab->cab/dot_general | solution.py:22
  85.3 34.2 %copy.17 = f32[256,128,256]{2,1,0:T(8,128)} copy(f32[256,128,256]{0,2,1:T(8,128)} %convolution_bitcast_fusion) | data formatting | bytes 67108864
  119.4 0.0 reduce-scatter.13.cloned.1.call-done
  119.4 0.0 reduce-scatter.7.cloned.1.call-done
  119.4 0.0 copy-done.1
Async XLA Ops:
  7.2 1.2 copy-start
  7.2 18.6 %reduce-scatter.9.cloned.1.call-start = ((), (), s32[]{:S(2)}) async-start(), calls=%async_computation.5 | async-start | bytes 393216 | tf_op jit(solution)/shard_map/reduce_scatter | solution.py:19
  11.2 40.1 %reduce-scatter.11.cloned.1.call-start = ((), (), s32[]{:S(2)}) async-start(), calls=%async_computation.6 | async-start | bytes 655360 | tf_op jit(solution)/shard_map/reduce_scatter | solution.py:21
  28.2 91.2 %reduce-scatter.13.cloned.1.call-start = ((), (), s32[]{:S(2)}) async-start(), calls=%async_computation.7 | async-start | bytes 163840
  31.3 88.1 %reduce-scatter.7.cloned.1.call-start = ((), (), s32[]{:S(2)}) async-start(), calls=%async_computation.4 | async-start | bytes 589824 | tf_op jit(solution)/shard_map/reduce_scatter | solution.py:17
  54.3 65.1 %copy-start.1 = (f32[512,512]{1,0:T(8,128)S(1)}, f32[512,512]{1,0:T(8,128)}, u32[]{:S(2)}) copy-start(f32[512,512]{1,0:T(8,128)} %param.13) | copy-start | bytes 3145732
Sparse Core Ops, SparseCore 0:
  11.4 14.3 reduce-scatter.8
  28.7 21.7 reduce-scatter.10
  53.6 17.8 reduce-scatter.12
  74.2 30.9 reduce-scatter.6
